TPU v7x, 32 devices: a whole 2x2x4 slice. The times are simulated.
32 devices in a mesh: vx: 2 (over x), vy: 4 (over y, core), scan: 4 (over z).
Axes of the slice: x: 2, y: 2, z: 4, core: 2. Of those that a mesh axis runs over, the one named last changes fastest.
Arguments:
- volume: bfloat16 [2, 64, 256, 256], P(None, 'vx', 'vy'), may hold values from -6 to 6
- tile_matrix: bfloat16 [4, 2, 8, 1024, 128], P('scan', 'vx', 'vy'), may hold values from -0.09375 to 0.09375
- tile_offset: int32 [4, 2, 8], P('scan', 'vx', 'vy'), may hold values from 0 to 384
- patch_count: int32 [4, 8], P('scan', ('vx', 'vy')), may hold values from 1 to 3, as said below
- scan_position: int32 [4, 8, 3, 2], P('scan', ('vx', 'vy')), may hold values from 0 to 256, as said below
- measured: float32 [4, 8, 3, 256, 256], P('scan', ('vx', 'vy')), may hold values from 0.2 to 5
- illumination: float32 [2, 256, 256], replicated, may hold values from -6 to 6
Outputs:
- change: float32 [2, 64, 256, 256], P(None, 'vx', 'vy', 'scan')
Inputs may be any that keep to these rules, and one draw needn't show every extreme that they name: `patch_count`: an owner's slots below its count hold measured patches, the others are unused; at every angle some owner holds 3. `scan_position`: column 0 is a patch's first detector column, 0 to 256; column 1 its first row, 0 to 0.
All inputs are finite; a program needn't handle non-finite values.
Results may differ from a plain program's by a relative error of at most 0.0085.
Values may be sent and summed in bfloat16 or wider, within the bound.
No kernel may reach another device: no remote copies, remote signals or barrier semaphores. Data moves between devices by JAX's collectives and lax.ppermute only.
A program may use at most 64 MiB of HBM per device.

v0:
```python
import math

import jax
import jax.numpy as jnp
from jax import lax
from jax.sharding import PartitionSpec as P

TILE = 32
NZ = 256
U = 512
TU = 128
PATCH_SIDE = 256


ABSORPTION = 0.2
STEP_LENGTH = 0.003


def dft_tables(length):
    counter = jnp.arange(length, dtype=jnp.int32)
    product = counter[:, None] * counter[None, :] % length
    radians = product.astype(jnp.float32) * (2.0 * math.pi / length)
    scaling = 1.0 / math.sqrt(length)
    return (jnp.cos(radians) * scaling, jnp.sin(radians) * scaling)


def matmul(left, right):
    return jnp.dot(left, right, precision=lax.Precision.HIGHEST)


def patch_misfit(window, illumination, intensity, cosine_table, sine_table):
    amplitude = jnp.exp(-ABSORPTION * window[1])
    trans_re = amplitude * jnp.cos(window[0])
    trans_im = amplitude * jnp.sin(window[0])
    exit_re = illumination[0] * trans_re - illumination[1] * trans_im
    exit_im = illumination[0] * trans_im + illumination[1] * trans_re
    half_re = matmul(cosine_table, exit_re) + matmul(sine_table, exit_im)
    half_im = matmul(cosine_table, exit_im) - matmul(sine_table, exit_re)
    far_re = matmul(half_re, cosine_table) + matmul(half_im, sine_table)
    far_im = matmul(half_im, cosine_table) - matmul(half_re, sine_table)
    residue = far_re * far_re + far_im * far_im - intensity
    return jnp.sum(residue * residue)


def place_patch(summed_total, slope, corner):
    anchor = (jnp.zeros((), jnp.int32), corner[0], corner[1])
    before = lax.dynamic_slice(summed_total, anchor, slope.shape)
    return lax.dynamic_update_slice(summed_total, before + slope, anchor)


def patch_term(
    summed_total, projected_field, corner, intensity, illumination, cosine_table, sine_table
):
    anchor = (jnp.zeros((), jnp.int32), corner[0], corner[1])
    window = lax.dynamic_slice(projected_field, anchor, (2, PATCH_SIDE, PATCH_SIDE))
    slope = jax.grad(patch_misfit)(window, illumination, intensity, cosine_table, sine_table)
    return place_patch(summed_total, slope, corner)


def brick_tiles(field):
    components, width_x, width_y, depth_cells = field.shape
    blocks = field.reshape(components, width_x // TILE, TILE, width_y // TILE, TILE, depth_cells)
    blocks = blocks.transpose(1, 3, 0, 2, 4, 5)
    return blocks.reshape(-1, components, TILE * TILE, depth_cells)


def tiles_brick(blocks, width_x, width_y):
    components = blocks.shape[1]
    depth_cells = blocks.shape[3]
    shaped = blocks.reshape(width_x // TILE, width_y // TILE, components, TILE, TILE, depth_cells)
    return shaped.transpose(2, 0, 3, 1, 4, 5).reshape(components, width_x, width_y, depth_cells)


def partial_projection(current, matrices, offsets):
    blocks = brick_tiles(current)
    tile_parts = jnp.einsum("tku,tckz->tcuz", matrices, blocks, preferred_element_type=jnp.float32)
    summed_total = jnp.zeros((2, U, NZ), jnp.float32)
    for tile_index in range(tile_parts.shape[0]):
        anchor = (jnp.zeros((), jnp.int32), offsets[tile_index], jnp.zeros((), jnp.int32))
        before = lax.dynamic_slice(summed_total, anchor, tile_parts.shape[1:])
        summed_total = lax.dynamic_update_slice(
            summed_total, before + tile_parts[tile_index], anchor
        )
    return summed_total


def cut_windows(image, offsets):

    def cut_window(offset):
        anchor = (jnp.zeros((), jnp.int32), offset, jnp.zeros((), jnp.int32))
        return lax.dynamic_slice(image, anchor, (2, TU, NZ))

    return jax.vmap(cut_window)(offsets)


def back_tiles(matrices, windows, width_x, width_y):
    blocks = jnp.einsum("tku,tcuz->tckz", matrices, windows, preferred_element_type=jnp.float32)
    return tiles_brick(blocks, width_x, width_y)


def per_device(
    volume, tile_matrix, tile_offset, patch_count, scan_position, measured, illumination
):
    cosine_table, sine_table = dft_tables(PATCH_SIDE)
    matrices = tile_matrix[0].reshape(-1, TILE * TILE, TU)
    offsets = tile_offset[0].reshape(-1)
    live_count = patch_count[0, 0]
    positions = scan_position[0, 0]
    intensity_values = measured[0, 0]
    width_x = volume.shape[1]
    width_y = volume.shape[2]
    slab_depth = NZ // lax.axis_size("scan")
    slab_start = lax.axis_index("scan") * slab_depth

    def own_slot(slot_index, running, projected_field):
        return patch_term(
            running,
            projected_field,
            positions[slot_index],
            intensity_values[slot_index],
            illumination,
            cosine_table,
            sine_table,
        )

    iterate = lax.dynamic_slice_in_dim(volume, slab_start, slab_depth, 3).astype(jnp.float32)
    projected_field = lax.psum(partial_projection(volume, matrices, offsets), ("vx", "vy"))
    image = lax.psum(
        lax.fori_loop(
            0,
            live_count,
            lambda slot_index, running: own_slot(slot_index, running, projected_field),
            jnp.zeros_like(projected_field),
        ),
        ("vx", "vy"),
    )
    windows = cut_windows(image, offsets).astype(jnp.bfloat16)
    slope = back_tiles(matrices, windows, width_x, width_y)
    slope_sum = lax.psum_scatter(
        slope.astype(jnp.bfloat16), "scan", scatter_dimension=3, tiled=True
    ).astype(jnp.float32)
    iterate = iterate - STEP_LENGTH * slope_sum
    return iterate - lax.dynamic_slice_in_dim(volume, slab_start, slab_depth, 3).astype(jnp.float32)


def solution(mesh):
    in_specs = (
        P(None, "vx", "vy", None),
        P("scan", "vx", "vy", None, None),
        P("scan", "vx", "vy"),
        P("scan", ("vx", "vy")),
        P("scan", ("vx", "vy"), None, None),
        P("scan", ("vx", "vy"), None, None, None),
        P(),
    )
    out_specs = P(None, "vx", "vy", "scan")
    return jax.shard_map(
        per_device, mesh=mesh, in_specs=in_specs, out_specs=out_specs, check_vma=False
    )
```

profile of v0, /device:TPU:0, one launch (start us, length us, event | category | flops | bytes accessed | tf_op | source)
XLA Modules:
  0.0 324.6 jit_solution(10603027786342075903)
XLA Ops:
  10.4 1.8 copy.25
  14.7 1.6 dynamic_update_slice.10
  16.5 1.6 dynamic_update_slice.11
  19.4 59.3 %all-reduce.6.cloned.1.call-done = f32[2,512,256]{1,2,0:T(8,128)} async-done(((f32[2,512,256]{1,2,0:T(8,128)}), f32[2,512,256]{1,2,0:T(8,128)}) %all-reduce.6.cloned.1.call-update) | async-done | bytes 1048592 | tf_op jit(solution)/shard_map/psum | solution.py:127
  79.9 51.8 %while.12 = (s32[]{:T(128)}, f32[2,512,256]{2,0,1:T(2,128)}, s32[]{:T(128)}, s32[3,2]{0,1:T(2,128)S(1)}, f32[2,512,256]{1,2,0:T(8,128)}, /*index=5*/f32[2,256,25...) while((s32[]{:T(128)}, f32[2,512,256]{2,0,1:T(2,128)}, ...), condition=%wide.region_2.3_spmd.clone.clone, body=%wide.region_1.2_spmd.clone.clone.sunk | while | flops 3240427520 | bytes 30671164 | solution.py:129
  101.0 2.2 fusion.184
  106.0 1.5 fusion.186
  108.8 1.4 convolution_add_fusion.9
  110.2 1.5 convolution_subtract_fusion.5
  111.7 1.5 fusion.188
  113.1 2.4 add_multiply_fusion.3
  121.1 1.5 fusion.190
  122.6 1.5 fusion.192
  124.1 1.5 fusion.193
  125.5 2.4 fusion.194
  131.7 112.3 %all-reduce.7 = bf16[2,512,256]{2,0,1:T(2,128)(2,1)S(1)} all-reduce(f32[2,512,256]{2,0,1:T(2,128)} %get-tuple-element.94), channel_id=1, replica_groups=mesh['vx'=2,'vy'=4,'scan'=4] {'vx','vy'}, use_global_device_ids=true, to_apply=%region_3.4 | all-reduce | flops 262144 | bytes 1572864 | tf_op jit(solution)/shard_map/psum | solution.py:128
  245.9 2.6 copy.30
  248.5 1.8 copy.31
  250.3 6.7 %copy.34 = bf16[2,32,64,256]{2,1,0,3:T(8,128)(2,1)} copy(bf16[2,32,64,256]{3,2,1,0:T(8,128)(2,1)S(1)} %bitcast.209) | data formatting | bytes 4194304
  257.0 6.6 %reshape.60 = bf16[256,4096]{1,0:T(8,128)(2,1)} reshape(bf16[256,2,32,64]{3,2,1,0:T(8,128)(2,1)} %bitcast.208) | data formatting | bytes 4194304
  263.6 45.0 %reduce-scatter.4.cloned.1.call-done = bf16[64,4096]{1,0:T(8,128)(2,1)} async-done(((bf16[256,4096]{1,0:T(8,128)(2,1)}), bf16[64,4096]{1,0:T(8,128)(2,1)}) %reduce-scatter.4.cloned.1.call-update) | async-done | bytes 524304
  308.6 2.7 reshape.61
  311.4 2.9 copy.35
  314.3 3.1 subtract_subtract_fusion
  (45 shorter events, 19.9 us)
Async XLA Ops:
  6.5 5.7 %copy-start = (bf16[1,1,2,1024,128]{4,3,2,1,0:T(8,128)(2,1)S(1)}, bf16[1,1,2,1024,128]{4,3,2,1,0:T(8,128)(2,1)}, u32[]{:S(2)}) copy-start(bf16[1,1,2,1024,128]{4,3,2,1,0:T(8,128)(2,1)} %param.10) | copy-start | bytes 1572868
  6.5 72.2 %all-reduce.6.cloned.1.call-start = ((), (), s32[]{:S(2)}) async-start(), calls=%async_computation.1 | async-start | bytes 2097152 | tf_op jit(solution)/shard_map/psum | solution.py:127
  13.2 6.0 %copy-start.5 = (f32[2,256,256]{2,1,0:T(8,128)S(1)}, f32[2,256,256]{2,1,0:T(8,128)}, u32[]{:S(2)}) copy-start(f32[2,256,256]{2,1,0:T(8,128)} %param.15) | copy-start | bytes 1572868
  14.7 4.7 %copy-start.7 = (s32[1,1,2]{2,1,0:T(1,128)S(1)}, s32[1,1,2]{2,1,0:T(1,128)}, u32[]{:S(2)}) copy-start(s32[1,1,2]{2,1,0:T(1,128)} %param.11) | copy-start | bytes 28
  16.3 63.6 %copy-start.6 = (s32[1,1,3,2]{2,3,1,0:T(2,128)S(1)}, s32[1,1,3,2]{2,3,1,0:T(2,128)}, u32[]{:S(2)}) copy-start(s32[1,1,3,2]{2,3,1,0:T(2,128)} %param.13) | copy-start | bytes 76
  18.1 1.0 copy-start.3
  19.1 289.5 %reduce-scatter.4.cloned.1.call-start = ((), (), s32[]{:S(2)}) async-start(), calls=%async_computation.2 | async-start | bytes 2621440
  121.1 4.4 %copy-start.1 = (f32[2,512,256]{1,2,0:T(8,128)S(1)}, f32[2,512,256]{1,2,0:T(8,128)}, u32[]{:S(2)}) copy-start(f32[2,512,256]{1,2,0:T(8,128)} %get-tuple-element.294) | copy-start | bytes 3145732 | tf_op jit(solution)/shard_map/while
  125.5 3.6 %copy-start.2 = (f32[2,512,256]{2,0,1:T(2,128)S(1)}, f32[2,512,256]{2,0,1:T(2,128)}, u32[]{:S(2)}) copy-start(f32[2,512,256]{2,0,1:T(2,128)} %get-tuple-element.279) | copy-start | bytes 3145732 | tf_op jit(solution)/shard_map/while
  263.6 50.7 %copy-start.4 = (bf16[2,32,64,256]{3,2,1,0:T(8,128)(2,1)S(1)}, bf16[2,32,64,256]{3,2,1,0:T(8,128)(2,1)}, u32[]{:S(2)}) copy-start(bf16[2,32,64,256]{3,2,1,0:T(8,128)(2,1)} %param.9) | copy-start | bytes 6291460
Sparse Core Ops, SparseCore 0:
  19.2 59.4 all-reduce.5
  263.7 44.8 reduce-scatter.3
where the time goes:
time: 324 us; the launch traced here: 325 us
  blocking collectives  112 us (35%)
  waiting for transfers between devices  104 us (32%)
  local copies, waits for them, and re-layouts  35.6 us (11%)
  matrix products  26.3 us (8%)
  loops' own time  21.5 us (7%)
  between operations  17.9 us (6%)
  other arithmetic  6.69 us (2%)
    psum x1, blocking collectives, per_device(): lax.psum(lax.fori_loop(0, live_count, lambda slot_index, running: own_slo...  112 us
    psum x1, waiting for transfers between devices, per_device(): lax.psum(partial_projection(volume, matrices, offsets), ('vx', 'vy'))  59.3 us
    unnamed x3, waiting for transfers between devices  45 us
    dot_general x16, matrix products, matmul(): return jnp.dot(left, right, precision=lax.Precision.HIGHEST)  24.6 us
    another operation x1, loops' own time, per_device(): lax.fori_loop(0, live_count, lambda slot_index, running: own_slot(slot_in...  21.5 us
    unnamed x17, local copies, waits for them, and re-layouts  20.1 us
  transfers between devices with their start and end apart: 2, of which 2 were waited for; matrix products, arithmetic and copies ran while one was open for 0% of the time, Pallas kernels for 0%

commit v1 on v0

v1 whole, which is shorter than its diff:
```python
import functools
import math

import jax
import jax.numpy as jnp
import numpy as np
from jax import lax
from jax.experimental import pallas as pl
from jax.experimental.pallas import tpu as pltpu
from jax.sharding import PartitionSpec as P

TILE = 32
U = 512
ABSORPTION = 0.2
STEP_LENGTH = 0.003
SUBLANES = 8
VMEM_LIMIT = 56 * 1024 * 1024

F32 = jnp.float32
BF16 = jnp.bfloat16
F16 = jnp.float16


def dft_block(length):
    counter = np.arange(length)
    radians = (np.outer(counter, counter) % length) * (2.0 * math.pi / length)
    scaling = 1.0 / math.sqrt(length)
    cosine = np.cos(radians) * scaling
    sine = np.sin(radians) * scaling
    return np.block([[cosine, sine], [-sine, cosine]])


def high_low(table):
    high = table.astype(np.float32).astype(BF16)
    low = (table - high.astype(np.float64)).astype(np.float32).astype(BF16)
    return high, low


def half_pi_parts():
    rest = math.pi / 2
    parts = []
    for bits in (8, 10, 11):
        unit = 2.0 ** (math.floor(math.log2(rest)) - bits + 1)
        part = math.floor(rest / unit) * unit
        parts.append(part)
        rest -= part
    return parts + [rest]


HALF_PI_PARTS = half_pi_parts()


def sine_cosine(angle):
    turns = jnp.round(angle * (2.0 / math.pi))
    rest = angle
    for part in HALF_PI_PARTS:
        rest = rest - turns * part
    quadrant = turns.astype(jnp.int32)
    square = rest * rest
    sine = rest * (
        1.0 + square * (-1 / 6 + square * (1 / 120 + square * (-1 / 5040 + square * (1 / 362880))))
    )
    cosine = 1.0 + square * (
        -0.5 + square * (1 / 24 + square * (-1 / 720 + square * (1 / 40320 - square * (1 / 3628800))))
    )
    swap = (quadrant & 1) == 1
    sine_out = jnp.where(swap, cosine, sine)
    cosine_out = jnp.where(swap, sine, cosine)
    sine_out = jnp.where((quadrant & 2) == 2, -sine_out, sine_out)
    cosine_out = jnp.where(((quadrant + 1) & 2) == 2, -cosine_out, cosine_out)
    return sine_out, cosine_out


def load_rows(ref, lead, start, count):
    base = pl.multiple_of((start // SUBLANES) * SUBLANES, SUBLANES)
    shift = start - base
    block = ref[lead, pl.ds(base, count + SUBLANES), :]
    width = block.shape[-1]
    groups = count // SUBLANES
    turned = pltpu.roll(block.reshape(groups + 1, SUBLANES, width), SUBLANES - shift, 1)
    row = lax.broadcasted_iota(jnp.int32, (groups, SUBLANES, width), 1)
    return jnp.where(row < SUBLANES - shift, turned[:-1], turned[1:]).reshape(count, width)


def add_rows(ref, lead, start, values):
    count, width = values.shape
    groups = count // SUBLANES
    base = pl.multiple_of((start // SUBLANES) * SUBLANES, SUBLANES)
    shift = start - base
    turned = pltpu.roll(values.reshape(groups, SUBLANES, width), shift, 1)
    blank = jnp.zeros((1, SUBLANES, width), values.dtype)
    row = lax.broadcasted_iota(jnp.int32, (groups + 1, SUBLANES, width), 1)
    moved = jnp.where(
        row >= shift,
        jnp.concatenate([turned, blank], 0),
        jnp.concatenate([blank, turned], 0),
    )
    ref[lead, pl.ds(base, count + SUBLANES), :] += moved.reshape(count + SUBLANES, width)


def dot(left, right):
    return jnp.dot(left, right, preferred_element_type=F32)


def split(value):
    high = value.astype(BF16)
    return high, (value - high.astype(F32)).astype(BF16)


class Plan:
    def __init__(self, mesh):
        self.slabs = mesh.shape["scan"]
        self.plane = mesh.shape["vx"] * mesh.shape["vy"]
        bits = self.plane.bit_length() - 1
        self.slab_bits = self.slabs.bit_length() - 1
        assert 1 << bits == self.plane and 1 << self.slab_bits == self.slabs
        groups = [(0, 1)]
        low = 1
        while low < bits:
            size = min(2, bits - low)
            groups.append((low, size))
            low += size
        self.groups = groups
        order = [0]
        for low, size in groups:
            order = [known | (digit << low) for known in order for digit in range(1 << size)]
        self.order = order

    def slab_digit(self, index):
        return (index >> 1) & (self.slabs - 1)

    def chunk_digit(self, index):
        return (index & 1) | ((index >> (1 + self.slab_bits)) << 1)


def plane_send(value, plan, mask):
    pairs = [(index, index ^ mask) for index in range(plan.plane)]
    return lax.ppermute(value, ("vx", "vy"), pairs)


def scatter_stage(keep, sends, plan, group):
    low = group[0]
    total = keep
    for digit, send in sends:
        total = total + plane_send(send, plan, digit << low).astype(F32)
    return total


def split_stage(total, group, dtype):
    parts = total.reshape((1 << group[1], -1) + total.shape[1:])
    return parts[0], [(digit, parts[digit].astype(dtype)) for digit in range(1, 1 << group[1])]


def gather_pieces(piece, plan):
    held = [(0, piece)]
    for low, size in reversed(plan.groups):
        arrived = []
        for digit in range(1, 1 << size):
            arrived += [
                (mask | (digit << low), plane_send(value, plan, digit << low)) for mask, value in held
            ]
        held = held + arrived
    return held


def project_kernel(plan, place_ref, offset_ref, volume_ref, matrix_ref, out_ref, image_ref):
    tiles, _, reach = matrix_ref.shape
    components, _, width_y, depth = volume_ref.shape
    tiles_y = width_y // TILE
    me = place_ref[0]
    image_ref[...] = jnp.zeros_like(image_ref)
    for tile in range(tiles):
        tile_x, tile_y = divmod(tile, tiles_y)
        rows = slice(tile_x * TILE, (tile_x + 1) * TILE)
        columns = slice(tile_y * TILE, (tile_y + 1) * TILE)
        for part in range(components):
            block = volume_ref[part, rows, columns, :].reshape(TILE * TILE, depth)
            cast = lax.dot_general(
                matrix_ref[tile], block, (((0,), (0,)), ((), ())), preferred_element_type=F32
            )
            add_rows(image_ref, part, offset_ref[tile], cast)
    length = out_ref.shape[1]
    per_part = U // length
    for spot, mask in enumerate(plan.order):
        piece = me ^ mask
        start = pl.multiple_of((piece % per_part) * length, SUBLANES)
        out_ref[spot] = image_ref[piece // per_part, pl.ds(start, length), :]


def patch_kernel(
    plan, passes, place_ref, count_ref, corner_ref, *refs
):
    pieces = refs[: plan.plane]
    (measured_ref, illumination_ref, left_high, left_low, right_high, right_low,
     keep_ref, send_ref, field_ref, image_ref) = refs[plan.plane:]
    forward, backward = passes
    me = place_ref[0]
    angle = place_ref[1]
    slots, side, _ = measured_ref.shape
    length = pieces[0].shape[0]
    per_part = U // length
    for (mask, piece_ref) in zip(plan.order, pieces):
        piece = me ^ mask
        start = pl.multiple_of((piece % per_part) * length, SUBLANES)
        field_ref[piece // per_part, pl.ds(start, length), :] = piece_ref[...]
    image_ref[...] = jnp.zeros_like(image_ref)

    def left(high, low, value, count):
        if count == 1:
            return dot(high[...], value.astype(BF16))
        upper, lower = split(value)
        total = dot(high[...], upper) + dot(low[...], upper)
        return total + dot(high[...], lower) if count == 3 else total

    def right(value, high, low, count):
        if count == 1:
            return dot(value.astype(BF16), high[...])
        upper, lower = split(value)
        total = dot(upper, high[...]) + dot(upper, low[...])
        return total + dot(lower, high[...]) if count == 3 else total

    def slot_step(slot, carry):
        start = corner_ref[slot]
        phase = load_rows(field_ref, 0, start, side)
        absorbed = load_rows(field_ref, 1, start, side)
        amplitude = jnp.exp(-ABSORPTION * absorbed)
        sine, cosine = sine_cosine(phase)
        trans_re = amplitude * cosine
        trans_im = amplitude * sine
        exit_re = illumination_ref[0] * trans_re - illumination_ref[1] * trans_im
        exit_im = illumination_ref[0] * trans_im + illumination_ref[1] * trans_re
        stacked = jnp.concatenate([exit_re, exit_im], axis=0)
        half = left(left_high, left_low, stacked, forward)
        half = jnp.concatenate([half[:side], half[side:]], axis=1)
        far = right(half, right_high, right_low, forward)
        far_re = far[:, :side]
        far_im = far[:, side:]
        residue = 4.0 * (far_re * far_re + far_im * far_im - measured_ref[slot])
        slope = jnp.concatenate([residue * far_re, residue * far_im], axis=1)
        slope = right(slope, left_high, left_low, backward)
        slope = jnp.concatenate([slope[:, :side], slope[:, side:]], axis=0)
        slope = left(right_high, right_low, slope, backward)
        slope_re = slope[:side]
        slope_im = slope[side:]
        add_rows(image_ref, 0, start, exit_re * slope_im - exit_im * slope_re)
        add_rows(image_ref, 1, start, -ABSORPTION * (exit_re * slope_re + exit_im * slope_im))
        return carry

    lax.fori_loop(0, count_ref[0], slot_step, 0)

    lanes = keep_ref.shape[-1]
    half_lanes = lanes // 2
    chunk_rows = keep_ref.shape[1]
    kept = keep_ref.shape[0]
    column = lax.broadcasted_iota(jnp.int32, (chunk_rows, lanes), 1)
    for spot, mask in enumerate(plan.order):
        target = me ^ mask
        slab = angle ^ plan.slab_digit(target)
        rows = pl.ds(pl.multiple_of(plan.chunk_digit(target) * chunk_rows, SUBLANES), chunk_rows)
        across = pl.ds(pl.multiple_of((slab // 2) * lanes, 128), lanes)
        odd = (slab % 2) * half_lanes
        first = pltpu.roll(image_ref[0, rows, across], odd, 1)
        second = pltpu.roll(image_ref[1, rows, across], half_lanes - odd, 1)
        packed = jnp.where(column < half_lanes, first, second)
        if spot < kept:
            keep_ref[spot] = packed
        else:
            send_ref[spot - kept] = packed.astype(BF16)


def back_kernel(plan, place_ref, offset_ref, *refs):
    pieces = refs[: plan.plane]
    own_ref, near_ref, inner_two, inner_three, outer_two, outer_three, out_ref, window_ref = refs[
        plan.plane:
    ]
    me = place_ref[0]
    angle = place_ref[1]
    inside = (angle > 0) & (angle < plan.slabs - 1)
    tiles, cells, reach = own_ref.shape
    tiles_y = out_ref.shape[2] // TILE
    rows, lanes = pieces[0].shape
    depth = lanes // 2
    for mask, piece_ref in zip(plan.order, pieces):
        source = me ^ mask
        start = pl.multiple_of(plan.chunk_digit(source) * rows, SUBLANES)
        window_ref[plan.slab_digit(source), pl.ds(start, rows), :] = piece_ref[...].astype(F32)
    for tile in range(tiles):
        two = jnp.where(inside, inner_two[tile], outer_two[tile])
        three = jnp.where(inside, inner_three[tile], outer_three[tile])
        weights = jnp.concatenate([own_ref[tile], near_ref[tile], two, three], axis=1)
        windows = jnp.concatenate(
            [
                load_rows(window_ref, other, offset_ref[other, tile], reach).astype(BF16)
                for other in range(plan.slabs)
            ],
            axis=0,
        )
        block = dot(weights, windows) * (-STEP_LENGTH)
        tile_x, tile_y = divmod(tile, tiles_y)
        at_x = slice(tile_x * TILE, (tile_x + 1) * TILE)
        at_y = slice(tile_y * TILE, (tile_y + 1) * TILE)
        out_ref[0, at_x, at_y, :] = block[:, :depth].reshape(TILE, TILE, depth)
        out_ref[1, at_x, at_y, :] = block[:, depth:].reshape(TILE, TILE, depth)


def vmem(count):
    return [pl.BlockSpec(memory_space=pltpu.VMEM)] * count


def smem(count):
    return [pl.BlockSpec(memory_space=pltpu.SMEM)] * count


def kernel_call(body, out_shape, scalars, arrays, scratch):
    outs = len(out_shape) if isinstance(out_shape, list) else 1
    return pl.pallas_call(
        body,
        out_shape=out_shape,
        in_specs=smem(len(scalars)) + vmem(len(arrays)),
        out_specs=vmem(outs) if outs > 1 else vmem(1)[0],
        scratch_shapes=scratch,
        compiler_params=pltpu.CompilerParams(vmem_limit_bytes=VMEM_LIMIT),
    )(*scalars, *arrays)


def scan_send(value, pairs):
    return lax.ppermute(value, "scan", pairs)


def gather_matrices(matrices, slabs):
    swap = [(index, index ^ 1) for index in range(slabs)]
    middle = [(1, 2), (2, 1)]
    outward = [(1, 0), (2, 3)]
    near = scan_send(matrices, swap)
    inner_three = scan_send(matrices, middle)
    inner_two = scan_send(near, middle)
    outer_two = scan_send(inner_three, outward)
    outer_three = scan_send(inner_two, outward)
    return near, inner_two, inner_three, outer_two, outer_three


def per_device(
    plan, axis_names, volume, tile_matrix, tile_offset, patch_count, scan_position, measured, illumination
):
    slabs = plan.slabs
    assert slabs == 4
    reach = tile_matrix.shape[-1]
    matrices = tile_matrix[0].reshape(-1, TILE * TILE, reach)
    offsets = tile_offset[0].reshape(-1)
    side = measured.shape[-1]
    depth = volume.shape[-1]
    me = lax.axis_index(("vx", "vy"))
    angle = lax.axis_index("scan")
    place = jnp.stack([me, angle]).astype(jnp.int32)
    near, inner_two, inner_three, outer_two, outer_three = gather_matrices(matrices, slabs)
    all_offsets = jnp.stack(
        [offsets]
        + [
            scan_send(offsets, [(index, index ^ mask) for index in range(slabs)])
            for mask in range(1, slabs)
        ]
    )

    length = 2 * U // plan.plane
    projected = kernel_call(
        functools.partial(project_kernel, plan),
        jax.ShapeDtypeStruct((plan.plane, length, depth), F32),
        [place, offsets],
        [volume, matrices],
        [pltpu.VMEM((2, U + SUBLANES, depth), F32)],
    )
    for group in plan.groups:
        keep, sends = split_stage(projected, group, F16)
        projected = scatter_stage(keep, sends, plan, group)
    pieces = dict(gather_pieces(projected[0].astype(F16), plan))
    pieces = [pieces[mask].astype(F32) for mask in plan.order]

    table = dft_block(side)
    tables = [jnp.asarray(item) for item in high_low(table) + high_low(table.T)]
    chunk_rows = U * slabs // plan.plane
    lanes = 2 * depth // slabs
    halves = plan.plane // 2
    keep, send = kernel_call(
        functools.partial(patch_kernel, plan, (3, 1)),
        [
            jax.ShapeDtypeStruct((halves, chunk_rows, lanes), F32),
            jax.ShapeDtypeStruct((halves, chunk_rows, lanes), BF16),
        ],
        [place, patch_count[0], scan_position[0, 0, :, 0]],
        pieces + [measured[0, 0], illumination] + tables,
        [pltpu.VMEM((2, U + SUBLANES, depth), F32)] * 2,
    )
    total = scatter_stage(keep, [(1, send)], plan, plan.groups[0])
    for group in plan.groups[1:]:
        keep, sends = split_stage(total, group, BF16)
        total = scatter_stage(keep, sends, plan, group)
    route = [
        (index * slabs + at, index * slabs + (at ^ plan.slab_digit(index)))
        for index in range(plan.plane)
        for at in range(slabs)
    ]
    moved = lax.ppermute(total[0].astype(BF16), axis_names, route)
    windows = dict(gather_pieces(moved, plan))
    return kernel_call(
        functools.partial(back_kernel, plan),
        jax.ShapeDtypeStruct(volume.shape[:3] + (depth // slabs,), F32),
        [place, all_offsets],
        [windows[mask] for mask in plan.order]
        + [matrices, near, inner_two, inner_three, outer_two, outer_three],
        [pltpu.VMEM((slabs, U + SUBLANES, lanes), F32)],
    )


def solution(mesh):
    in_specs = (
        P(None, "vx", "vy", None),
        P("scan", "vx", "vy", None, None),
        P("scan", "vx", "vy"),
        P("scan", ("vx", "vy")),
        P("scan", ("vx", "vy"), None, None),
        P("scan", ("vx", "vy"), None, None, None),
        P(),
    )
    out_specs = P(None, "vx", "vy", "scan")
    body = functools.partial(per_device, Plan(mesh), tuple(mesh.axis_names))
    return jax.shard_map(body, mesh=mesh, in_specs=in_specs, out_specs=out_specs, check_vma=False)
```

time: 324 us -> 106 us (0.33)
  blocking collectives: 112 us -> 0 us
  waiting for transfers between devices: 104 us -> 12.2 us
  starting transfers between devices: 0.04 us -> 67 us
  local copies, waits for them, and re-layouts: 35.6 us -> 2.12 us
  matrix products: 26.3 us -> 0 us
  loops' own time: 21.5 us -> 0 us
  between operations: 17.9 us -> 0.94 us
  Pallas kernels: 0 us -> 14 us
  other arithmetic: 6.69 us -> 10 us
    psum x1 -> x0, blocking collectives: 112 us -> none  [per_device(): lax.psum(lax.fori_loop(0, live_count, lambda slot_index, running: own_slo...]
    ppermute x0 -> x31, starting transfers between devices: none -> 67 us  [the longest x22 39.6 us: plane_send(): return lax.ppermute(value, ('vx', 'vy'), pairs)]
    psum x1 -> x0, waiting for transfers between devices: 59.3 us -> none  [per_device(): lax.psum(partial_projection(volume, matrices, offsets), ('vx', 'vy'))]
    unnamed x3 -> x0, waiting for transfers between devices: 45 us -> none
    dot_general x18 -> x0, matrix products: 26.3 us -> none  [the longest x16 24.6 us: matmul(): return jnp.dot(left, right, precision=lax.Precision.HIGHEST)]
    another operation x1 -> x0, loops' own time: 21.5 us -> none  [per_device(): lax.fori_loop(0, live_count, lambda slot_index, running: own_slot(slot_in...]
    unnamed x17 -> x32, local copies, waits for them, and re-layouts: 20.1 us -> 1.56 us
    pallas_call x0 -> x3, Pallas kernels: none -> 14 us  [kernel_call(): pl.pallas_call(body, out_shape=out_shape, in_specs=smem(len(scalars)) + v...]
  transfers between devices with their start and end apart: 2 -> 31, of which waited for: 2 -> 11; matrix products, arithmetic and copies ran while one was open for 0% -> 7% of each run, Pallas kernels for 0% -> 6%
where the time goes in v1:
time: 106 us
  starting transfers between devices  67 us (63%)
  Pallas kernels  14 us (13%)
  waiting for transfers between devices  12.2 us (12%)
  other arithmetic  10 us (9%)
  local copies, waits for them, and re-layouts  2.12 us (2%)
    ppermute x22, starting transfers between devices, plane_send(): return lax.ppermute(value, ('vx', 'vy'), pairs)  39.6 us
    ppermute x8, starting transfers between devices, scan_send(): return lax.ppermute(value, 'scan', pairs)  26.8 us
    pallas_call x3, Pallas kernels, kernel_call(): pl.pallas_call(body, out_shape=out_shape, in_specs=smem(len(scalars)) + v...  14 us
    ppermute x22, waiting for transfers between devices, plane_send(): return lax.ppermute(value, ('vx', 'vy'), pairs)  12.2 us
    convert_element_type x8, other arithmetic, per_device(): pieces = [pieces[mask].astype(F32) for mask in plan.order]  5.34 us
    another operation x3, other arithmetic  3.38 us
  transfers between devices with their start and end apart: 31, of which 11 were waited for; matrix products, arithmetic and copies ran while one was open for 7% of the time, Pallas kernels for 6%

profile of v1, /device:TPU:0, one launch (start us, length us, event | category | flops | bytes accessed | tf_op | source)
XLA Modules:
  0.0 106.3 jit_solution(314344836726608843)
XLA Ops:
  0.7 3.3 %shard_map.109 = f32[8,128,256]{2,1,0:T(8,128)} custom-call(s32[2]{0:T(128)} %pad_add_fusion.1.place_ref, s32[2]{0:T(128)} %bitcast.23, bf16[2,32,64,256]{3,2,1,0:T(8,128)(2,1)} %volume_ref.1, bf16[2,1024,128]{2,1,0:T(8,128)(2,1)} %bitcast.18), custom_call_target="tpu_custom_call" | custom-call | tf_op jit(solution)/shard_map/pallas_call | solution.py:316
  3.9 1.1 %slice_convert_fusion = f16[4,128,256]{2,1,0:T(8,128)(2,1)S(1)} fusion(f32[8,128,256]{2,1,0:T(8,128)} %shard_map.109), kind=kLoop, calls=%fused_computation | loop fusion | flops 131072 | bytes 786432 | tf_op jit(solution)/shard_map/convert.6
  5.6 1.2 %collective-permute-done.3 = f16[4,128,256]{2,1,0:T(8,128)(2,1)S(1)} collective-permute-done((f16[4,128,256]{2,1,0:T(8,128)(2,1)S(1)}, f16[4,128,256]{2,1,0:T(8,128)(2,1)S(1)}, u32[]{:S(2)}, u32[]{:S(2)}) %collective-permute-start.3) | collective-permute-done | bytes 262176 | tf_op jit(solution)/shard_map/ppermute | solution.py:138
  6.8 1.1 %fusion.11 = (f16[4,128,256]{2,1,0:T(8,128)(2,1)S(1)}, f32[4,128,256]{2,1,0:T(8,128)S(1)}) fusion(f16[4,128,256]{2,1,0:T(8,128)(2,1)S(1)} %collective-permute-done.3, f32[8,128,256]{2,1,0:T(8,128)} %shard_map.109), kind=kLoop, calls=%fused_computation.18 | loop fusion | flops 393216 | bytes 1572864 | tf_op jit(solution)/shard_map/convert.5
  8.0 2.9 %collective-permute-start.4 = (f16[1,128,256]{2,1,0:T(8,128)(2,1)S(1)}, f16[1,128,256]{2,1,0:T(8,128)(2,1)S(1)}, u32[]{:S(2)}, u32[]{:S(2)}) collective-permute-start(f16[1,128,256]{2,1,0:T(8,128)(2,1)S(1)} %get-tuple-element.18), channel_id=1, source_target_pairs={{0,8},{4,12},{8,0},{12,4},{16,24},{20,28},{24,16},{28,20},{1,9},{5... | collective-permute-start | bytes 196616 | tf_op jit(solution)/shard_map/ppermute | solution.py:138
  10.9 1.4 %collective-permute-start.6 = (f16[1,128,256]{2,1,0:T(8,128)(2,1)S(1)}, f16[1,128,256]{2,1,0:T(8,128)(2,1)S(1)}, u32[]{:S(2)}, u32[]{:S(2)}) collective-permute-start(f16[1,128,256]{2,1,0:T(8,128)(2,1)S(1)} %get-tuple-element.19), channel_id=1, source_target_pairs={{0,24},{4,28},{8,16},{12,20},{16,8},{20,12},{24,0},{28,4},{1,25},{... | collective-permute-start | bytes 196616 | tf_op jit(solution)/shard_map/ppermute | solution.py:138
  12.5 1.7 %collective-permute-done.4 = f16[1,128,256]{2,1,0:T(8,128)(2,1)S(1)} collective-permute-done((f16[1,128,256]{2,1,0:T(8,128)(2,1)S(1)}, f16[1,128,256]{2,1,0:T(8,128)(2,1)S(1)}, u32[]{:S(2)}, u32[]{:S(2)}) %collective-permute-start.4) | collective-permute-done | bytes 65568 | tf_op jit(solution)/shard_map/ppermute | solution.py:138
  14.1 2.5 %collective-permute-done.6 = f16[1,128,256]{2,1,0:T(8,128)(2,1)S(1)} collective-permute-done((f16[1,128,256]{2,1,0:T(8,128)(2,1)S(1)}, f16[1,128,256]{2,1,0:T(8,128)(2,1)S(1)}, u32[]{:S(2)}, u32[]{:S(2)}) %collective-permute-start.6) | collective-permute-done | bytes 65568 | tf_op jit(solution)/shard_map/ppermute | solution.py:138
  17.4 1.9 %collective-permute-start.9 = (f16[128,256]{1,0:T(8,128)(2,1)S(1)}, f16[128,256]{1,0:T(8,128)(2,1)S(1)}, u32[]{:S(2)}, u32[]{:S(2)}) collective-permute-start(f16[128,256]{1,0:T(8,128)(2,1)S(1)} %get-tuple-element.12), channel_id=1, source_target_pairs={{0,24},{4,28},{8,16},{12,20},{16,8},{20,12},{24,0},{28,4},{1,25},{... | collective-permute-start | bytes 196616 | tf_op jit(solution)/shard_map/ppermute | solution.py:138
  20.9 1.6 %collective-permute-start.26 = (bf16[2,1024,128]{2,1,0:T(8,128)(2,1)S(1)}, bf16[2,1024,128]{2,1,0:T(8,128)(2,1)S(1)}, u32[]{:S(2)}, u32[]{:S(2)}) collective-permute-start(bf16[2,1024,128]{2,1,0:T(8,128)(2,1)S(1)} %bitcast.20), channel_id=1, source_target_pairs={{0,1},{1,0},{2,3},{3,2},{4,5},{5,4},{6,7},{7,6},{8,9},{9,8},{10,11... | collective-permute-start | bytes 1572872 | tf_op jit(solution)/shard_map/ppermute | solution.py:327
  30.4 6.5 %shard_map.110 = (f32[4,256,128]{2,1,0:T(8,128)}, bf16[4,256,128]{2,1,0:T(8,128)(2,1)}) custom-call(s32[2]{0:T(128)} %pad_add_fusion.1.place_ref, s32[1]{0:T(128)} %bitcast.17.count_ref, s32[3]{0:T(128)} %slice_bitcast_fusion.corner_ref, f32[128,256]{1,0:T(8,128)} %get-tuple-element.11.refs_0_, f32[128,256]{1,0:T(8,128)} %convert_element_type.86.refs_1_, ...), custom_call_target="tpu_custom_call" | custom-call | tf_op jit(solution)/shard_map/pallas_call | solution.py:316
  36.9 6.0 %collective-permute-start.14 = (bf16[4,256,128]{2,1,0:T(8,128)(2,1)}, bf16[4,256,128]{2,1,0:T(8,128)(2,1)S(1)}, u32[]{:S(2)}, u32[]{:S(2)}) collective-permute-start(bf16[4,256,128]{2,1,0:T(8,128)(2,1)} %get-tuple-element.8), channel_id=1, source_target_pairs={{0,4},{4,0},{8,12},{12,8},{16,20},{20,16},{24,28},{28,24},{1,5},{5... | collective-permute-start | bytes 786440 | tf_op jit(solution)/shard_map/ppermute | solution.py:138
  44.3 1.1 %fusion.8 = (bf16[4,256,128]{2,1,0:T(8,128)(2,1)S(1)}, f32[4,256,128]{2,1,0:T(8,128)S(1)}) fusion(f32[4,256,128]{2,1,0:T(8,128)} %get-tuple-element.7, bf16[4,256,128]{2,1,0:T(8,128)(2,1)S(1)} %collective-permute-done.14), kind=kLoop, calls=%fused_computation.16 | loop fusion | flops 393216 | bytes 1572864 | tf_op jit(solution)/shard_map/convert.2
  46.1 1.9 %collective-permute-start.17 = (bf16[1,256,128]{2,1,0:T(8,128)(2,1)S(1)}, bf16[1,256,128]{2,1,0:T(8,128)(2,1)S(1)}, u32[]{:S(2)}, u32[]{:S(2)}) collective-permute-start(bf16[1,256,128]{2,1,0:T(8,128)(2,1)S(1)} %get-tuple-element.16), channel_id=1, source_target_pairs={{0,24},{4,28},{8,16},{12,20},{16,8},{20,12},{24,0},{28,4},{1,25},{... | collective-permute-start | bytes 196616 | tf_op jit(solution)/shard_map/ppermute | solution.py:138
  49.0 1.3 %collective-permute-start.29 = (bf16[2,1024,128]{2,1,0:T(8,128)(2,1)S(1)}, bf16[2,1024,128]{2,1,0:T(8,128)(2,1)S(1)}, u32[]{:S(2)}, u32[]{:S(2)}) collective-permute-start(bf16[2,1024,128]{2,1,0:T(8,128)(2,1)S(1)} %collective-permute-done.28.refs_11_), channel_id=1, source_target_pairs={{1,0},{2,3},{5,4},{6,7},{9,8},{10,11},{13,12},{14,15},{17,16},{18,... | collective-permute-start | bytes 1572872 | tf_op jit(solution)/shard_map/ppermute | solution.py:327
  50.3 1.3 %collective-permute-start.30 = (bf16[2,1024,128]{2,1,0:T(8,128)(2,1)S(1)}, bf16[2,1024,128]{2,1,0:T(8,128)(2,1)S(1)}, u32[]{:S(2)}, u32[]{:S(2)}) collective-permute-start(bf16[2,1024,128]{2,1,0:T(8,128)(2,1)S(1)} %collective-permute-done.27.refs_10_), channel_id=1, source_target_pairs={{1,0},{2,3},{5,4},{6,7},{9,8},{10,11},{13,12},{14,15},{17,16},{18,... | collective-permute-start | bytes 1572872 | tf_op jit(solution)/shard_map/ppermute | solution.py:327
  53.3 3.5 %collective-permute-start.2 = (s32[2]{0:T(128)S(1)}, s32[2]{0:T(128)S(1)}, u32[]{:S(2)}, u32[]{:S(2)}) collective-permute-start(s32[2]{0:T(128)S(1)} %bitcast.24), channel_id=1, source_target_pairs={{0,3},{1,2},{2,1},{3,0},{4,7},{5,6},{6,5},{7,4},{8,11},{9,10},{10,... | collective-permute-start | bytes 32 | tf_op jit(solution)/shard_map/ppermute | solution.py:327
  56.8 15.7 %collective-permute-start.1 = (s32[2]{0:T(128)S(1)}, s32[2]{0:T(128)S(1)}, u32[]{:S(2)}, u32[]{:S(2)}) collective-permute-start(s32[2]{0:T(128)S(1)} %bitcast.25), channel_id=1, source_target_pairs={{0,2},{1,3},{2,0},{3,1},{4,6},{5,7},{6,4},{7,5},{8,10},{9,11},{10,... | collective-permute-start | bytes 32 | tf_op jit(solution)/shard_map/ppermute | solution.py:327
  72.4 2.1 %collective-permute-start = (s32[2]{0:T(128)S(1)}, s32[2]{0:T(128)S(1)}, u32[]{:S(2)}, u32[]{:S(2)}) collective-permute-start(s32[2]{0:T(128)S(1)} %bitcast.26), channel_id=1, source_target_pairs={{0,1},{1,0},{2,3},{3,2},{4,5},{5,4},{6,7},{7,6},{8,9},{9,8},{10,11... | collective-permute-start | bytes 32 | tf_op jit(solution)/shard_map/ppermute | solution.py:327
  74.6 10.6 %collective-permute-start.21 = (bf16[256,128]{1,0:T(8,128)(2,1)S(1)}, bf16[256,128]{1,0:T(8,128)(2,1)S(1)}, u32[]{:S(2)}, u32[]{:S(2)}) collective-permute-start(bf16[256,128]{1,0:T(8,128)(2,1)S(1)} %collective-permute-done.18.refs_0_), channel_id=1, source_target_pairs={{0,24},{4,28},{8,16},{12,20},{16,8},{20,12},{24,0},{28,4},{1,25},{... | collective-permute-start | bytes 196616 | tf_op jit(solution)/shard_map/ppermute | solution.py:138
  85.1 9.8 %collective-permute-start.20 = (bf16[256,128]{1,0:T(8,128)(2,1)S(1)}, bf16[256,128]{1,0:T(8,128)(2,1)S(1)}, u32[]{:S(2)}, u32[]{:S(2)}) collective-permute-start(bf16[256,128]{1,0:T(8,128)(2,1)S(1)} %collective-permute-done.18.refs_0_), channel_id=1, source_target_pairs={{0,16},{4,20},{8,24},{12,28},{16,0},{20,4},{24,8},{28,12},{1,17},{... | collective-permute-start | bytes 196616 | tf_op jit(solution)/shard_map/ppermute | solution.py:138
  95.6 2.2 %collective-permute-done.20.refs_2_ = bf16[256,128]{1,0:T(8,128)(2,1)S(1)} collective-permute-done((bf16[256,128]{1,0:T(8,128)(2,1)S(1)}, bf16[256,128]{1,0:T(8,128)(2,1)S(1)}, u32[]{:S(2)}, u32[]{:S(2)}) %collective-permute-start.20) | collective-permute-done | bytes 65568 | tf_op jit(solution)/shard_map/ppermute | solution.py:138
  97.8 1.3 %collective-permute-done.19.refs_1_ = bf16[256,128]{1,0:T(8,128)(2,1)S(1)} collective-permute-done((bf16[256,128]{1,0:T(8,128)(2,1)S(1)}, bf16[256,128]{1,0:T(8,128)(2,1)S(1)}, u32[]{:S(2)}, u32[]{:S(2)}) %collective-permute-start.19) | collective-permute-done | bytes 65568 | tf_op jit(solution)/shard_map/ppermute | solution.py:138
  102.0 4.3 %shard_map.111 = f32[2,32,64,64]{3,2,1,0:T(8,128)} custom-call(s32[2]{0:T(128)} %pad_add_fusion.1.place_ref, s32[4,2]{1,0:T(4,128)} %pad_add_fusion.offset_ref, bf16[256,128]{1,0:T(8,128)(2,1)} %copy-done.6, bf16[256,128]{1,0:T(8,128)(2,1)} %copy-done.10, bf16[256,128]{1,0:T(8,128)(2,1)} %copy-done.9, bf16[256,128]{1,0:T(8,128)(2,1)} %copy-done.8, ...), custom_call_target="tpu_custom_call" | custom-call | tf_op jit(solution)/shard_map/pallas_call | solution.py:316
  (90 shorter events, 19.1 us)
Async XLA Ops:
  8.0 6.2 %collective-permute-start.4 = (f16[1,128,256]{2,1,0:T(8,128)(2,1)S(1)}, f16[1,128,256]{2,1,0:T(8,128)(2,1)S(1)}, u32[]{:S(2)}, u32[]{:S(2)}) collective-permute-start(f16[1,128,256]{2,1,0:T(8,128)(2,1)S(1)} %get-tuple-element.18), channel_id=1, source_target_pairs={{0,8},{4,12},{8,0},{12,4},{16,24},{20,28},{24,16},{28,20},{1,9},{5... | collective-permute-start | bytes 196616 | tf_op jit(solution)/shard_map/ppermute | solution.py:138
  10.9 5.8 %collective-permute-start.6 = (f16[1,128,256]{2,1,0:T(8,128)(2,1)S(1)}, f16[1,128,256]{2,1,0:T(8,128)(2,1)S(1)}, u32[]{:S(2)}, u32[]{:S(2)}) collective-permute-start(f16[1,128,256]{2,1,0:T(8,128)(2,1)S(1)} %get-tuple-element.19), channel_id=1, source_target_pairs={{0,24},{4,28},{8,16},{12,20},{16,8},{20,12},{24,0},{28,4},{1,25},{... | collective-permute-start | bytes 196616 | tf_op jit(solution)/shard_map/ppermute | solution.py:138
  12.3 4.3 %collective-permute-start.5 = (f16[1,128,256]{2,1,0:T(8,128)(2,1)S(1)}, f16[1,128,256]{2,1,0:T(8,128)(2,1)S(1)}, u32[]{:S(2)}, u32[]{:S(2)}) collective-permute-start(f16[1,128,256]{2,1,0:T(8,128)(2,1)S(1)} %get-tuple-element.20), channel_id=1, source_target_pairs={{0,16},{4,20},{8,24},{12,28},{16,0},{20,4},{24,8},{28,12},{1,17},{... | collective-permute-start | bytes 196616 | tf_op jit(solution)/shard_map/ppermute | solution.py:138
  17.4 5.3 %collective-permute-start.9 = (f16[128,256]{1,0:T(8,128)(2,1)S(1)}, f16[128,256]{1,0:T(8,128)(2,1)S(1)}, u32[]{:S(2)}, u32[]{:S(2)}) collective-permute-start(f16[128,256]{1,0:T(8,128)(2,1)S(1)} %get-tuple-element.12), channel_id=1, source_target_pairs={{0,24},{4,28},{8,16},{12,20},{16,8},{20,12},{24,0},{28,4},{1,25},{... | collective-permute-start | bytes 196616 | tf_op jit(solution)/shard_map/ppermute | solution.py:138
  20.9 22.7 %collective-permute-start.26 = (bf16[2,1024,128]{2,1,0:T(8,128)(2,1)S(1)}, bf16[2,1024,128]{2,1,0:T(8,128)(2,1)S(1)}, u32[]{:S(2)}, u32[]{:S(2)}) collective-permute-start(bf16[2,1024,128]{2,1,0:T(8,128)(2,1)S(1)} %bitcast.20), channel_id=1, source_target_pairs={{0,1},{1,0},{2,3},{3,2},{4,5},{5,4},{6,7},{7,6},{8,9},{9,8},{10,11... | collective-permute-start | bytes 1572872 | tf_op jit(solution)/shard_map/ppermute | solution.py:327
  22.4 5.3 %collective-permute-start.10 = (f16[128,256]{1,0:T(8,128)(2,1)S(1)}, f16[128,256]{1,0:T(8,128)(2,1)S(1)}, u32[]{:S(2)}, u32[]{:S(2)}) collective-permute-start(f16[128,256]{1,0:T(8,128)(2,1)S(1)} %get-tuple-element.12), channel_id=1, source_target_pairs={{0,4},{4,0},{8,12},{12,8},{16,20},{20,16},{24,28},{28,24},{1,5},{5... | collective-permute-start | bytes 196616 | tf_op jit(solution)/shard_map/ppermute | solution.py:138
  22.6 5.7 %collective-permute-start.13 = (f16[128,256]{1,0:T(8,128)(2,1)S(1)}, f16[128,256]{1,0:T(8,128)(2,1)S(1)}, u32[]{:S(2)}, u32[]{:S(2)}) collective-permute-start(f16[128,256]{1,0:T(8,128)(2,1)S(1)} %collective-permute-done.9), channel_id=1, source_target_pairs={{0,4},{4,0},{8,12},{12,8},{16,20},{20,16},{24,28},{28,24},{1,5},{5... | collective-permute-start | bytes 196616 | tf_op jit(solution)/shard_map/ppermute | solution.py:138
  23.5 5.5 %collective-permute-start.12 = (f16[128,256]{1,0:T(8,128)(2,1)S(1)}, f16[128,256]{1,0:T(8,128)(2,1)S(1)}, u32[]{:S(2)}, u32[]{:S(2)}) collective-permute-start(f16[128,256]{1,0:T(8,128)(2,1)S(1)} %collective-permute-done.8), channel_id=1, source_target_pairs={{0,4},{4,0},{8,12},{12,8},{16,20},{20,16},{24,28},{28,24},{1,5},{5... | collective-permute-start | bytes 196616 | tf_op jit(solution)/shard_map/ppermute | solution.py:138
  24.5 5.2 %collective-permute-start.11 = (f16[128,256]{1,0:T(8,128)(2,1)S(1)}, f16[128,256]{1,0:T(8,128)(2,1)S(1)}, u32[]{:S(2)}, u32[]{:S(2)}) collective-permute-start(f16[128,256]{1,0:T(8,128)(2,1)S(1)} %collective-permute-done.7), channel_id=1, source_target_pairs={{0,4},{4,0},{8,12},{12,8},{16,20},{20,16},{24,28},{28,24},{1,5},{5... | collective-permute-start | bytes 196616 | tf_op jit(solution)/shard_map/ppermute | solution.py:138
  36.9 7.4 %collective-permute-start.14 = (bf16[4,256,128]{2,1,0:T(8,128)(2,1)}, bf16[4,256,128]{2,1,0:T(8,128)(2,1)S(1)}, u32[]{:S(2)}, u32[]{:S(2)}) collective-permute-start(bf16[4,256,128]{2,1,0:T(8,128)(2,1)} %get-tuple-element.8), channel_id=1, source_target_pairs={{0,4},{4,0},{8,12},{12,8},{16,20},{20,16},{24,28},{28,24},{1,5},{5... | collective-permute-start | bytes 786440 | tf_op jit(solution)/shard_map/ppermute | solution.py:138
  42.9 6.1 %collective-permute-start.28 = (bf16[2,1024,128]{2,1,0:T(8,128)(2,1)S(1)}, bf16[2,1024,128]{2,1,0:T(8,128)(2,1)S(1)}, u32[]{:S(2)}, u32[]{:S(2)}) collective-permute-start(bf16[2,1024,128]{2,1,0:T(8,128)(2,1)S(1)} %bitcast.21), channel_id=1, source_target_pairs={{1,2},{2,1},{5,6},{6,5},{9,10},{10,9},{13,14},{14,13},{17,18},{18,... | collective-permute-start | bytes 1572872 | tf_op jit(solution)/shard_map/ppermute | solution.py:327
  43.6 6.7 %collective-permute-start.27 = (bf16[2,1024,128]{2,1,0:T(8,128)(2,1)S(1)}, bf16[2,1024,128]{2,1,0:T(8,128)(2,1)S(1)}, u32[]{:S(2)}, u32[]{:S(2)}) collective-permute-start(bf16[2,1024,128]{2,1,0:T(8,128)(2,1)S(1)} %collective-permute-done.26.refs_9_), channel_id=1, source_target_pairs={{1,2},{2,1},{5,6},{6,5},{9,10},{10,9},{13,14},{14,13},{17,18},{18,... | collective-permute-start | bytes 1572872 | tf_op jit(solution)/shard_map/ppermute | solution.py:327
  45.5 6.2 %collective-permute-start.15 = (bf16[1,256,128]{2,1,0:T(8,128)(2,1)S(1)}, bf16[1,256,128]{2,1,0:T(8,128)(2,1)S(1)}, u32[]{:S(2)}, u32[]{:S(2)}) collective-permute-start(bf16[1,256,128]{2,1,0:T(8,128)(2,1)S(1)} %get-tuple-element.15), channel_id=1, source_target_pairs={{0,8},{4,12},{8,0},{12,4},{16,24},{20,28},{24,16},{28,20},{1,9},{5... | collective-permute-start | bytes 196616 | tf_op jit(solution)/shard_map/ppermute | solution.py:138
  46.1 5.6 %collective-permute-start.17 = (bf16[1,256,128]{2,1,0:T(8,128)(2,1)S(1)}, bf16[1,256,128]{2,1,0:T(8,128)(2,1)S(1)}, u32[]{:S(2)}, u32[]{:S(2)}) collective-permute-start(bf16[1,256,128]{2,1,0:T(8,128)(2,1)S(1)} %get-tuple-element.16), channel_id=1, source_target_pairs={{0,24},{4,28},{8,16},{12,20},{16,8},{20,12},{24,0},{28,4},{1,25},{... | collective-permute-start | bytes 196616 | tf_op jit(solution)/shard_map/ppermute | solution.py:138
  48.0 4.5 %collective-permute-start.16 = (bf16[1,256,128]{2,1,0:T(8,128)(2,1)S(1)}, bf16[1,256,128]{2,1,0:T(8,128)(2,1)S(1)}, u32[]{:S(2)}, u32[]{:S(2)}) collective-permute-start(bf16[1,256,128]{2,1,0:T(8,128)(2,1)S(1)} %get-tuple-element.17), channel_id=1, source_target_pairs={{0,16},{4,20},{8,24},{12,28},{16,0},{20,4},{24,8},{28,12},{1,17},{... | collective-permute-start | bytes 196616 | tf_op jit(solution)/shard_map/ppermute | solution.py:138
  49.0 51.4 %collective-permute-start.29 = (bf16[2,1024,128]{2,1,0:T(8,128)(2,1)S(1)}, bf16[2,1024,128]{2,1,0:T(8,128)(2,1)S(1)}, u32[]{:S(2)}, u32[]{:S(2)}) collective-permute-start(bf16[2,1024,128]{2,1,0:T(8,128)(2,1)S(1)} %collective-permute-done.28.refs_11_), channel_id=1, source_target_pairs={{1,0},{2,3},{5,4},{6,7},{9,8},{10,11},{13,12},{14,15},{17,16},{18,... | collective-permute-start | bytes 1572872 | tf_op jit(solution)/shard_map/ppermute | solution.py:327
  50.3 50.1 %collective-permute-start.30 = (bf16[2,1024,128]{2,1,0:T(8,128)(2,1)S(1)}, bf16[2,1024,128]{2,1,0:T(8,128)(2,1)S(1)}, u32[]{:S(2)}, u32[]{:S(2)}) collective-permute-start(bf16[2,1024,128]{2,1,0:T(8,128)(2,1)S(1)} %collective-permute-done.27.refs_10_), channel_id=1, source_target_pairs={{1,0},{2,3},{5,4},{6,7},{9,8},{10,11},{13,12},{14,15},{17,16},{18,... | collective-permute-start | bytes 1572872 | tf_op jit(solution)/shard_map/ppermute | solution.py:327
  53.2 41.7 %collective-permute-start.22 = (bf16[256,128]{1,0:T(8,128)(2,1)S(1)}, bf16[256,128]{1,0:T(8,128)(2,1)S(1)}, u32[]{:S(2)}, u32[]{:S(2)}) collective-permute-start(bf16[256,128]{1,0:T(8,128)(2,1)S(1)} %collective-permute-done.18.refs_0_), channel_id=1, source_target_pairs={{0,4},{4,0},{8,12},{12,8},{16,20},{20,16},{24,28},{28,24},{1,5},{5... | collective-permute-start | bytes 196616 | tf_op jit(solution)/shard_map/ppermute | solution.py:138
  53.3 19.2 %collective-permute-start.2 = (s32[2]{0:T(128)S(1)}, s32[2]{0:T(128)S(1)}, u32[]{:S(2)}, u32[]{:S(2)}) collective-permute-start(s32[2]{0:T(128)S(1)} %bitcast.24), channel_id=1, source_target_pairs={{0,3},{1,2},{2,1},{3,0},{4,7},{5,6},{6,5},{7,4},{8,11},{9,10},{10,... | collective-permute-start | bytes 32 | tf_op jit(solution)/shard_map/ppermute | solution.py:327
  56.8 17.8 %collective-permute-start.1 = (s32[2]{0:T(128)S(1)}, s32[2]{0:T(128)S(1)}, u32[]{:S(2)}, u32[]{:S(2)}) collective-permute-start(s32[2]{0:T(128)S(1)} %bitcast.25), channel_id=1, source_target_pairs={{0,2},{1,3},{2,0},{3,1},{4,6},{5,7},{6,4},{7,5},{8,10},{9,11},{10,... | collective-permute-start | bytes 32 | tf_op jit(solution)/shard_map/ppermute | solution.py:327
  72.4 12.7 %collective-permute-start = (s32[2]{0:T(128)S(1)}, s32[2]{0:T(128)S(1)}, u32[]{:S(2)}, u32[]{:S(2)}) collective-permute-start(s32[2]{0:T(128)S(1)} %bitcast.26), channel_id=1, source_target_pairs={{0,1},{1,0},{2,3},{3,2},{4,5},{5,4},{6,7},{7,6},{8,9},{9,8},{10,11... | collective-permute-start | bytes 32 | tf_op jit(solution)/shard_map/ppermute | solution.py:327
  74.6 21.1 %collective-permute-start.21 = (bf16[256,128]{1,0:T(8,128)(2,1)S(1)}, bf16[256,128]{1,0:T(8,128)(2,1)S(1)}, u32[]{:S(2)}, u32[]{:S(2)}) collective-permute-start(bf16[256,128]{1,0:T(8,128)(2,1)S(1)} %collective-permute-done.18.refs_0_), channel_id=1, source_target_pairs={{0,24},{4,28},{8,16},{12,20},{16,8},{20,12},{24,0},{28,4},{1,25},{... | collective-permute-start | bytes 196616 | tf_op jit(solution)/shard_map/ppermute | solution.py:138
  85.1 12.7 %collective-permute-start.20 = (bf16[256,128]{1,0:T(8,128)(2,1)S(1)}, bf16[256,128]{1,0:T(8,128)(2,1)S(1)}, u32[]{:S(2)}, u32[]{:S(2)}) collective-permute-start(bf16[256,128]{1,0:T(8,128)(2,1)S(1)} %collective-permute-done.18.refs_0_), channel_id=1, source_target_pairs={{0,16},{4,20},{8,24},{12,28},{16,0},{20,4},{24,8},{28,12},{1,17},{... | collective-permute-start | bytes 196616 | tf_op jit(solution)/shard_map/ppermute | solution.py:138
  94.9 4.3 %collective-permute-start.19 = (bf16[256,128]{1,0:T(8,128)(2,1)S(1)}, bf16[256,128]{1,0:T(8,128)(2,1)S(1)}, u32[]{:S(2)}, u32[]{:S(2)}) collective-permute-start(bf16[256,128]{1,0:T(8,128)(2,1)S(1)} %collective-permute-done.18.refs_0_), channel_id=1, source_target_pairs={{0,8},{4,12},{8,0},{12,4},{16,24},{20,28},{24,16},{28,20},{1,9},{5... | collective-permute-start | bytes 196616 | tf_op jit(solution)/shard_map/ppermute | solution.py:138
  (23 other events, 296.0 us)
